TPU v7x, 128 devices: a whole 4x4x4 slice. The times are simulated.
128 devices in a mesh: loc: 16 (over y, x), stream: 8 (over z, core).
Axes of the slice: x: 4, y: 4, z: 4, core: 2. Of those that a mesh axis runs over, the one named last changes fastest.
Arguments:
- latent: bfloat16 [49152, 1024], P(('loc', 'stream')), may hold values from -7 to 7
- observations: bfloat16 [8, 16, 16, 32, 1024], P('stream', 'loc'), may hold values from -7 to 7
- counts: int32 [8, 16, 16], P('stream', 'loc'), may hold values from 1 to 32, as said below
- cross_query: bfloat16 [1024, 1024], replicated, may hold values from -1 to 1
- cross_kv: bfloat16 [1024, 2048], replicated, may hold values from -1 to 1
- cross_out: bfloat16 [1024, 1024], replicated, may hold values from -0.1875 to 0.1875
- self_qkv: bfloat16 [1024, 3072], replicated, may hold values from -1 to 1
- self_out: bfloat16 [1024, 1024], replicated, may hold values from -0.1875 to 0.1875
- mlp_in: bfloat16 [1024, 4096], P(None, ('loc', 'stream')), may hold values from -0.1875 to 0.1875
- mlp_out: bfloat16 [1024, 4096], P(None, ('loc', 'stream')), may hold values from -0.09375 to 0.09375
Outputs:
- forecast: bfloat16 [49152, 1024], P(('loc', 'stream'))
Inputs may be any that keep to these rules, and one draw needn't show every extreme that they name: `counts`: slots 0 to count - 1 of a block hold observations and the rest are padding; for every stream some section receives 32 rows from every ingest shard.
All inputs are finite; a program needn't handle non-finite values.
Results may differ from a plain program's by a relative error of at most 0.013.
Values may be sent and summed in bfloat16 or wider, within the bound.
A program may use at most 192 MiB of HBM per device.

v0:
```python
import functools
import math

import jax
import jax.numpy as jnp
from jax import lax
from jax.experimental import pallas as pl
from jax.experimental.pallas import tpu as pltpu
from jax.sharding import Mesh
from jax.sharding import PartitionSpec as P

HEADS = 16
HEAD = 64
PAIR = 128
GROUPS = 8
WIN = 512
LOC = 16
CAP = 32
STREAM = ("s0", "s1")
LOC_STREAM = ("loc", "s0", "s1")
EPSILON = 1e-06
MASKED = -1e30
PADDING = 1e30
PADDING_FROM = 1e29
QSCALE = math.log2(math.e) / math.sqrt(HEAD)
MESH = pl.DeviceIdType.MESH
F32 = jnp.float32
BF16 = jnp.bfloat16
NT = (((1,), (1,)), ((), ()))
VMEM_LIMIT = 56 << 20


def params(**more):
    return pltpu.CompilerParams(vmem_limit_bytes=VMEM_LIMIT, **more)


def rms_norm(tensor):
    floats = tensor.astype(F32)
    return (floats * lax.rsqrt(jnp.mean(floats * floats, axis=-1, keepdims=True) + EPSILON)).astype(
        BF16
    )


def project_kernel(
    counts, obs, latent, wk, wv, wq, w_in, w_back, kv_out, q_out, column,
    xn, ln, send, recv,
):
    loc = lax.axis_index("loc")
    z = lax.axis_index("s0")
    core = lax.axis_index("s1")
    step = pl.program_id(0)

    @pl.when(step == 0)
    def _():
        barrier = pltpu.get_barrier_semaphore()
        for d in range(1, 4):
            pl.semaphore_signal(
                barrier, inc=1, device_id=(loc, lax.rem(z + d, 4), core), device_id_type=MESH
            )
        xn[...] = rms_norm(obs[...])
        ln[...] = rms_norm(latent[...])

        pl.semaphore_wait(barrier, 3)
        for at, part in enumerate((w_in, w_back)):
            pltpu.make_async_copy(part, column.at[z, at], recv).start()
            for d in range(1, 4):
                pltpu.make_async_remote_copy(
                    part, column.at[z, at], send, recv,
                    device_id=(loc, lax.rem(z + d, 4), core), device_id_type=MESH,
                ).start()

    q = (jnp.dot(ln[...], wq[...], preferred_element_type=F32) * QSCALE).astype(BF16)
    k = jnp.dot(xn[...], wk[...], preferred_element_type=F32)
    v = jnp.dot(xn[...], wv[...], preferred_element_type=F32)
    slot = lax.broadcasted_iota(jnp.int32, (CAP, PAIR), 0)
    for s in range(LOC):
        live = slot < counts[s]
        rows = slice(s * CAP, (s + 1) * CAP)
        for g in range(2):
            columns = slice(g * PAIR, (g + 1) * PAIR)
            kv_out[s, g, :, 0:PAIR] = jnp.where(live, k[rows, columns], PADDING).astype(BF16)
            kv_out[s, g, :, PAIR:] = jnp.where(live, v[rows, columns], PADDING).astype(BF16)
    for g in range(2):
        q_out[g] = q[:, g * PAIR : (g + 1) * PAIR]

    @pl.when(step == pl.num_programs(0) - 1)
    def _():
        sent = column.at[pl.ds(0, 3)]
        pltpu.make_async_copy(sent, sent, send).wait()
        pltpu.make_async_copy(column, column, recv).wait()


def project(counts, obs, latent, cross_kv, cross_query, w_in, w_back):
    rows, width = obs.shape
    nodes = latent.shape[0]
    step = 2 * PAIR
    steps = width // step
    return pl.pallas_call(
        project_kernel,
        grid=(steps,),
        out_shape=(
            jax.ShapeDtypeStruct((LOC, GROUPS, CAP, 2 * PAIR), BF16),
            jax.ShapeDtypeStruct((GROUPS, nodes, PAIR), BF16),
            jax.ShapeDtypeStruct((4, 2, *w_in.shape), BF16),
        ),
        in_specs=[
            pl.BlockSpec(memory_space=pltpu.SMEM),
            pl.BlockSpec((rows, width), lambda j: (0, 0)),
            pl.BlockSpec((nodes, width), lambda j: (0, 0)),
            pl.BlockSpec((width, step), lambda j: (0, j)),
            pl.BlockSpec((width, step), lambda j: (0, j + steps)),
            pl.BlockSpec((width, step), lambda j: (0, j)),
            pl.BlockSpec(memory_space=pl.ANY),
            pl.BlockSpec(memory_space=pl.ANY),
        ],
        out_specs=(
            pl.BlockSpec((LOC, 2, CAP, 2 * PAIR), lambda j: (0, j, 0, 0)),
            pl.BlockSpec((2, nodes, PAIR), lambda j: (j, 0, 0)),
            pl.BlockSpec(memory_space=pl.ANY),
        ),
        scratch_shapes=[
            pltpu.VMEM((rows, width), BF16),
            pltpu.VMEM((nodes, width), BF16),
            pltpu.SemaphoreType.DMA,
            pltpu.SemaphoreType.DMA,
        ],
        compiler_params=params(has_side_effects=True, collective_id=2),
        name="project",
    )(counts, obs, latent, cross_kv, cross_kv, cross_query, w_in, w_back)


def exchange_kernel(kv, q, kv_here, q_here, kv_send, kv_recv, q_send, q_recv):
    loc = lax.axis_index("loc")
    me = lax.axis_index("s0") * 2 + lax.axis_index("s1")
    mine = loc * GROUPS + me
    pltpu.make_async_copy(q.at[me], q_here.at[me], q_recv).start()
    pltpu.make_async_copy(kv.at[mine], kv_here.at[me * LOC + loc], kv_recv).start()

    @pl.loop(1, GROUPS)
    def _(d):
        to = lax.rem(me + d, GROUPS)
        pltpu.make_async_remote_copy(
            q.at[to],
            q_here.at[me],
            q_send,
            q_recv,
            device_id=(loc, to // 2, lax.rem(to, 2)),
            device_id_type=MESH,
        ).start()

    @pl.loop(1, LOC * GROUPS)
    def _(d):
        to = lax.rem(mine + d * 37, LOC * GROUPS)
        section = to // GROUPS
        group = lax.rem(to, GROUPS)
        pltpu.make_async_remote_copy(
            kv.at[to],
            kv_here.at[me * LOC + loc],
            kv_send,
            kv_recv,
            device_id=(section, group // 2, lax.rem(group, 2)),
            device_id_type=MESH,
        ).start()

    pltpu.make_async_copy(q.at[pl.ds(0, GROUPS - 1)], q_here.at[pl.ds(0, GROUPS - 1)], q_send).wait()
    pltpu.make_async_copy(q, q_here, q_recv).wait()

    sent = pl.ds(0, LOC * GROUPS - 1)
    pltpu.make_async_copy(kv.at[sent], kv_here.at[sent], kv_send).wait()
    pltpu.make_async_copy(kv_here, kv_here, kv_recv).wait()


def exchange(kv, q):
    return pl.pallas_call(
        exchange_kernel,
        out_shape=(
            jax.ShapeDtypeStruct(kv.shape, BF16),
            jax.ShapeDtypeStruct(q.shape, BF16),
        ),
        in_specs=[pl.BlockSpec(memory_space=pl.ANY)] * 2,
        out_specs=(pl.BlockSpec(memory_space=pl.ANY),) * 2,
        scratch_shapes=[pltpu.SemaphoreType.DMA] * 4,
        compiler_params=params(has_side_effects=True),
        name="exchange",
    )(kv, q)


def middle_kernel(
    latent, ctx, cross_out, self_qkv, after, q, kv,
    mixed, w_out, w_qkv, low, high, normed, w_sems, ctx_send, ctx_recv, send, recv,
):
    loc = lax.axis_index("loc")
    me = lax.axis_index("s0") * 2 + lax.axis_index("s1")
    flat = loc * GROUPS + me
    nodes, width = latent.shape
    half = low.shape[0]
    starts, ends = flat == 0, flat == LOC * GROUPS - 1
    outer_low = (me == 0) & jnp.logical_not(starts)
    outer_high = (me == GROUPS - 1) & jnp.logical_not(ends)

    def device(index):
        group = lax.rem(index, GROUPS)
        return index // GROUPS, group // 2, lax.rem(group, 2)

    load_out = pltpu.make_async_copy(cross_out, w_out, w_sems.at[0])
    load_qkv = pltpu.make_async_copy(self_qkv, w_qkv, w_sems.at[1])
    load_out.start()
    load_qkv.start()

    barrier = pltpu.get_barrier_semaphore()

    @pl.loop(1, GROUPS)
    def _(d):
        to = lax.rem(me + d, GROUPS)
        pl.semaphore_signal(
            barrier, inc=1, device_id=(loc, to // 2, lax.rem(to, 2)), device_id_type=MESH
        )

    @pl.when(outer_low)
    def _():
        pl.semaphore_signal(barrier, inc=1, device_id=device(flat - 1), device_id_type=MESH)

    @pl.when(outer_high)
    def _():
        pl.semaphore_signal(barrier, inc=1, device_id=device(flat + 1), device_id_type=MESH)

    pl.semaphore_wait(
        barrier, GROUPS - 1 + outer_low.astype(jnp.int32) + outer_high.astype(jnp.int32)
    )

    place = mixed.at[:, pl.ds(pl.multiple_of(me * PAIR, PAIR), PAIR)]

    @pl.loop(1, GROUPS)
    def _(d):
        to = lax.rem(me + d, GROUPS)
        pltpu.make_async_remote_copy(
            ctx.at[to],
            place,
            ctx_send,
            ctx_recv,
            device_id=(loc, to // 2, lax.rem(to, 2)),
            device_id_type=MESH,
        ).start()

    pltpu.make_async_copy(ctx.at[me], place, ctx_recv).start()

    @pl.when(starts)
    def _():
        low[...] = jnp.zeros_like(low)

    @pl.when(ends)
    def _():
        high[...] = jnp.zeros_like(high)

    load_out.wait()
    pltpu.make_async_copy(mixed, mixed, ctx_recv).wait()
    after[...] = (
        latent[...].astype(F32) + jnp.dot(mixed[...], w_out[...], preferred_element_type=F32)
    ).astype(BF16)

    down = pltpu.make_async_remote_copy(
        after.at[0:half], high, send.at[0], recv.at[1],
        device_id=device(jnp.maximum(flat - 1, 0)), device_id_type=MESH,
    )
    up = pltpu.make_async_remote_copy(
        after.at[nodes - half : nodes], low, send.at[1], recv.at[0],
        device_id=device(jnp.minimum(flat + 1, LOC * GROUPS - 1)), device_id_type=MESH,
    )
    pl.when(jnp.logical_not(starts))(down.start)
    pl.when(jnp.logical_not(ends))(up.start)

    normed[...] = rms_norm(after[...])
    load_qkv.wait()
    step = 512

    @pl.loop(0, width // step)
    def _(c):
        at = pl.ds(pl.multiple_of(c * step, step), step)
        found = jnp.dot(normed[...], w_qkv[:, at], preferred_element_type=F32)
        q[:, at] = (found * QSCALE).astype(BF16)

    def project(rows, to):
        @pl.loop(0, 2 * width // step)
        def _(c):
            at = pl.ds(pl.multiple_of(c * step, step), step)
            weights = w_qkv[:, pl.ds(pl.multiple_of(width + c * step, step), step)]
            kv[to, at] = jnp.dot(rows[...], weights, preferred_element_type=F32).astype(BF16)

    project(normed, slice(half, half + nodes))

    @pl.when(jnp.logical_not(starts))
    def _():
        pltpu.make_async_copy(low, low, recv.at[0]).wait()

    normed[0:half] = rms_norm(low[...])
    project(normed.at[0:half], slice(0, half))

    @pl.when(jnp.logical_not(ends))
    def _():
        pltpu.make_async_copy(high, high, recv.at[1]).wait()

    normed[0:half] = rms_norm(high[...])
    project(normed.at[0:half], slice(half + nodes, 2 * half + nodes))

    pl.when(jnp.logical_not(starts))(down.wait_send)
    pl.when(jnp.logical_not(ends))(up.wait_send)
    sent = ctx.at[pl.ds(0, GROUPS - 1)]
    pltpu.make_async_copy(sent, sent, ctx_send).wait()


def middle(latent, ctx, cross_out, self_qkv):
    nodes, width = latent.shape
    half = WIN // 2
    vmem = pl.BlockSpec(memory_space=pltpu.VMEM)
    away = pl.BlockSpec(memory_space=pl.ANY)
    return pl.pallas_call(
        middle_kernel,
        out_shape=(
            jax.ShapeDtypeStruct((nodes, width), BF16),
            jax.ShapeDtypeStruct((nodes, width), BF16),
            jax.ShapeDtypeStruct((nodes + WIN, 2 * width), BF16),
        ),
        in_specs=[vmem, away, away, away],
        out_specs=(vmem, vmem, vmem),
        scratch_shapes=[
            pltpu.VMEM((nodes, width), BF16),
            pltpu.VMEM((width, width), BF16),
            pltpu.VMEM((width, 3 * width), BF16),
            pltpu.VMEM((half, width), BF16),
            pltpu.VMEM((half, width), BF16),
            pltpu.VMEM((nodes, width), BF16),
            pltpu.SemaphoreType.DMA((2,)),
            pltpu.SemaphoreType.DMA,
            pltpu.SemaphoreType.DMA,
            pltpu.SemaphoreType.DMA((2,)),
            pltpu.SemaphoreType.DMA((2,)),
        ],
        compiler_params=params(has_side_effects=True, collective_id=1),
        name="middle",
    )(latent, ctx, cross_out, self_qkv)


PACK = 512
SIZES = (2048, 2304, 2560, 3072, 4096)
SPARE = 2048


def lane_max(scores, width):
    top = scores[:, 0:PAIR]
    for c in range(1, width // PAIR):
        top = jnp.maximum(top, scores[:, c * PAIR : (c + 1) * PAIR])
    return top


def pack_rows(kv, packed):
    groups = kv.shape[0] // PACK
    row = lax.broadcasted_iota(jnp.int32, (PACK, PACK), 0)
    column = lax.broadcasted_iota(jnp.int32, (PACK, PACK), 1)
    slot = lax.broadcasted_iota(jnp.int32, (PACK, 2 * PAIR), 0)
    earlier = (row < column).astype(BF16)
    lives = []
    for g in range(groups):
        key = kv[g * PACK : (g + 1) * PACK, 0:PAIR].astype(F32)
        lives.append(jnp.transpose(jnp.where(key < PADDING_FROM, 1.0, 0.0))[0:1, :])
    live = jnp.concatenate(lives, axis=0)
    before = jnp.dot(live.astype(BF16), earlier, preferred_element_type=F32)
    places = jnp.where(live > 0.5, before, -1.0).astype(jnp.int32)
    end = 0
    for g in range(groups):
        number = jnp.sum(live[g : g + 1, :]).astype(jnp.int32)
        pick = (places[g : g + 1, :] == row).astype(BF16)
        found = jnp.dot(pick, kv[g * PACK : (g + 1) * PACK, :], preferred_element_type=F32)
        packed[pl.ds(pl.multiple_of(end, 16), PACK), :] = jnp.where(
            slot < number, found, PADDING
        ).astype(BF16)
        end = end + (number + 15) // 16 * 16
    packed[pl.ds(pl.multiple_of(end, 16), SPARE), :] = jnp.full((SPARE, 2 * PAIR), PADDING, BF16)
    return end


def cross_kernel(kv, q, out, packed, k0, k1, v0, v1, s0, s1, length):
    block = q.shape[0]

    @pl.when(pl.program_id(0) == 0)
    def _():
        end = pack_rows(kv, packed)
        length[0] = end
        lane = lax.broadcasted_iota(jnp.int32, (PACK, PAIR), 1)
        low = lane < HEAD

        blocks = SIZES[-1] // PACK
        for size in SIZES[-2::-1]:
            blocks = jnp.where(end <= size, -(-size // PACK), blocks)

        @pl.loop(0, blocks)
        def _(b):
            at = pl.ds(pl.multiple_of(b * PACK, PACK), PACK)
            key = packed[at, 0:PAIR].astype(F32)
            value = packed[at, PAIR:].astype(F32)
            live = key < PADDING_FROM
            bias = jnp.where(live, 0.0, MASKED)
            key = jnp.where(live, key, 0.0)
            value = jnp.where(live, value, 0.0)
            first = jnp.where(low, key, jnp.where(lane == HEAD, bias, 0.0))
            second = jnp.where(low, jnp.where(lane == 0, bias, 0.0), key)
            k0[:, at] = jnp.transpose(first).astype(BF16)
            k1[:, at] = jnp.transpose(second).astype(BF16)
            v0[at, :] = jnp.where(low, value, 1.0).astype(BF16)
            v1[at, :] = jnp.where(low, 1.0, value).astype(BF16)

    end = length[0]

    def attend(size):
        lane = lax.broadcasted_iota(jnp.int32, (block, PAIR), 1)
        low = lane < HEAD
        both = q[...].astype(F32)
        q0 = jnp.where(low, both, jnp.where(lane == HEAD, 1.0, 0.0)).astype(BF16)
        q1 = jnp.where(low, jnp.where(lane == 0, 1.0, 0.0), both).astype(BF16)
        step = 512
        chunks = [slice(at, min(at + step, size)) for at in range(0, size, step)]
        lowest = jnp.full((block, PAIR), -3e38, F32)
        zero = jnp.zeros((block, PAIR), F32)

        def score(query, k, s, at, top):
            scores = jnp.dot(query, k[:, at], preferred_element_type=F32)
            s[:, at] = scores
            return jnp.maximum(top, lane_max(scores, at.stop - at.start))

        def mix(s, v, top, at, total):
            weights = jnp.exp2(s[:, at] - top).astype(BF16)
            return total + jnp.dot(weights, v[at, :], preferred_element_type=F32)

        top0, top1, t0, t1 = lowest, lowest, zero, zero
        for at in chunks:
            top0 = score(q0, k0, s0, at, top0)
        top0 = jnp.max(top0, axis=1, keepdims=True)
        for at in chunks:
            top1 = score(q1, k1, s1, at, top1)
            t0 = mix(s0, v0, top0, at, t0)
        top1 = jnp.max(top1, axis=1, keepdims=True)
        for at in chunks:
            t1 = mix(s1, v1, top1, at, t1)
        sums = pltpu.roll(jnp.where(low, t1, t0), HEAD, 1)
        out[...] = (jnp.where(low, t0, t1) / sums).astype(BF16)

    for below, size in zip((0, *SIZES[:-1]), SIZES):
        pl.when((end > below) & (end <= size))(functools.partial(attend, size))


def cross_attention(kv, q, block=512):
    rows = kv.shape[0]
    nodes = q.shape[0]
    return pl.pallas_call(
        cross_kernel,
        grid=(nodes // block,),
        out_shape=jax.ShapeDtypeStruct(q.shape, BF16),
        in_specs=[
            pl.BlockSpec((rows, 2 * PAIR), lambda j: (0, 0)),
            pl.BlockSpec((block, PAIR), lambda j: (j, 0)),
        ],
        out_specs=pl.BlockSpec((block, PAIR), lambda j: (j, 0)),
        scratch_shapes=[
            pltpu.VMEM((rows + SPARE, 2 * PAIR), BF16),
            pltpu.VMEM((PAIR, rows), BF16),
            pltpu.VMEM((PAIR, rows), BF16),
            pltpu.VMEM((rows, PAIR), BF16),
            pltpu.VMEM((rows, PAIR), BF16),
            pltpu.VMEM((block, rows), F32),
            pltpu.VMEM((block, rows), F32),
            pltpu.SMEM((1,), jnp.int32),
        ],
        compiler_params=params(),
        name="cross_attention",
    )(kv, q)


def window_kernel(block, q, key, value, out, bias):
    nodes = q.shape[0]
    window = key.shape[0]
    half = (window - nodes) // 2
    wide = block + 2 * half
    me = (lax.axis_index("loc") * 4 + lax.axis_index("s0")) * 2 + lax.axis_index("s1")

    @pl.when(pl.program_id(0) == 0)
    def _():
        first = jnp.where(me == 0, half, 0)
        last = jnp.where(me == LOC * GROUPS - 1, half + nodes, window)
        row = lax.broadcasted_iota(jnp.int32, (block, wide), 0)
        column = lax.broadcasted_iota(jnp.int32, (block, wide), 1)
        near = (column >= row) & (column <= row + 2 * half)
        for b in range(nodes // block):
            there = (column + b * block >= first) & (column + b * block < last)
            bias[b] = jnp.where(near & there, 0.0, MASKED)

    values = value[...].astype(F32)
    low_values = lax.broadcasted_iota(jnp.int32, values.shape, 1) < HEAD
    v0 = jnp.where(low_values, values, 1.0).astype(BF16)
    v1 = jnp.where(low_values, 1.0, values).astype(BF16)
    low = lax.broadcasted_iota(jnp.int32, (block, PAIR), 1) < HEAD
    for b in range(nodes // block):
        both = q[b * block : (b + 1) * block, :].astype(F32)
        q0 = jnp.where(low, both, 0.0).astype(BF16)
        q1 = jnp.where(low, 0.0, both).astype(BF16)
        near = slice(b * block, b * block + wide)
        a0 = lax.dot_general(q0, key[near, :], NT, preferred_element_type=F32) + bias[b]
        a1 = lax.dot_general(q1, key[near, :], NT, preferred_element_type=F32) + bias[b]
        p0 = jnp.exp2(a0 - jnp.max(a0, axis=1, keepdims=True)).astype(BF16)
        p1 = jnp.exp2(a1 - jnp.max(a1, axis=1, keepdims=True)).astype(BF16)
        t0 = jnp.dot(p0, v0[near], preferred_element_type=F32)
        t1 = jnp.dot(p1, v1[near], preferred_element_type=F32)
        sums = pltpu.roll(jnp.where(low, t1, t0), HEAD, 1)
        out[b * block : (b + 1) * block, :] = (jnp.where(low, t0, t1) / sums).astype(BF16)


def window_attention(q, kv, block=192):
    nodes = q.shape[0]
    window = kv.shape[0]
    return pl.pallas_call(
        functools.partial(window_kernel, block),
        grid=(GROUPS,),
        out_shape=jax.ShapeDtypeStruct(q.shape, BF16),
        in_specs=[
            pl.BlockSpec((nodes, PAIR), lambda j: (0, j)),
            pl.BlockSpec((window, PAIR), lambda j: (0, j)),
            pl.BlockSpec((window, PAIR), lambda j: (0, j + GROUPS)),
        ],
        out_specs=pl.BlockSpec((nodes, PAIR), lambda j: (0, j)),
        scratch_shapes=[pltpu.VMEM((nodes // block, block, block + window - nodes), F32)],
        compiler_params=params(),
        name="window_attention",
    )(q, kv, kv)


def tail_kernel(
    ctx, before, self_out, weights, out,
    w_in, w_back, x, mine, other, total, part, got, w_sems, send, recv,
):
    loc = lax.axis_index("loc")
    z = lax.axis_index("s0")
    core = lax.axis_index("s1")
    chunks, devices = w_in.shape[0], w_in.shape[1]
    sibling = functools.partial(
        pltpu.make_async_remote_copy, device_id=(loc, z, 1 - core), device_id_type=MESH
    )

    def load(c):
        at = pl.ds(c * devices, devices)
        return (
            pltpu.make_async_copy(weights.at[at, 0], w_in.at[c], w_sems.at[0, c]),
            pltpu.make_async_copy(weights.at[at, 1], w_back.at[c], w_sems.at[1, c]),
        )

    for c in range(chunks):
        for copy in load(c):
            copy.start()
    barrier = pltpu.get_barrier_semaphore()
    pl.semaphore_signal(barrier, inc=1, device_id=(loc, z, 1 - core), device_id_type=MESH)

    mixed = jnp.dot(ctx[...], self_out[...], preferred_element_type=F32)
    after = (before[...].astype(F32) + mixed).astype(BF16)
    x[...] = after
    mine[...] = rms_norm(after)
    pl.semaphore_wait(barrier, 1)
    give = sibling(mine, other, send.at[0], recv.at[0])
    give.start()

    def mlp(rows, c):
        wide = devices * w_in.shape[2]
        first = w_in[c].reshape(wide, w_in.shape[3])
        second = w_back[c].reshape(wide, w_back.shape[3])
        hidden = lax.dot_general(rows[...], first, NT, preferred_element_type=F32)
        hidden = jax.nn.gelu(hidden, approximate=True).astype(BF16)
        return jnp.dot(hidden, second, preferred_element_type=F32)

    for copy in load(0):
        copy.wait()
    total[...] = mlp(mine, 0)
    give.wait_recv()
    part[...] = mlp(other, 0)
    for c in range(1, chunks):
        for copy in load(c):
            copy.wait()

    @pl.loop(1, chunks)
    def _(c):
        part[...] += mlp(other, c)

    back = sibling(part, got, send.at[1], recv.at[1])
    back.start()

    @pl.loop(1, chunks)
    def _(c):
        total[...] += mlp(mine, c)

    back.wait_recv()
    out[...] = (x[...].astype(F32) + (total[...] + got[...])).astype(BF16)
    give.wait_send()
    back.wait_send()


def tail(ctx, before, self_out, weights, chunks=4):
    nodes, width = ctx.shape
    devices, _, units, _ = weights.shape
    vmem = pl.BlockSpec(memory_space=pltpu.VMEM)
    block = (chunks, devices // chunks, units, width)
    return pl.pallas_call(
        tail_kernel,
        out_shape=jax.ShapeDtypeStruct(ctx.shape, BF16),
        in_specs=[vmem, vmem, vmem, pl.BlockSpec(memory_space=pl.ANY)],
        out_specs=vmem,
        scratch_shapes=[
            pltpu.VMEM(block, BF16),
            pltpu.VMEM(block, BF16),
            pltpu.VMEM((nodes, width), BF16),
            pltpu.VMEM((nodes, width), BF16),
            pltpu.VMEM((nodes, width), BF16),
            pltpu.VMEM((nodes, width), F32),
            pltpu.VMEM((nodes, width), F32),
            pltpu.VMEM((nodes, width), F32),
            pltpu.SemaphoreType.DMA((2, chunks)),
            pltpu.SemaphoreType.DMA((2,)),
            pltpu.SemaphoreType.DMA((2,)),
        ],
        compiler_params=params(has_side_effects=True, collective_id=3),
        name="tail",
    )(ctx, before, self_out, weights)


def shards(
    latent,
    observations,
    counts,
    cross_query,
    cross_kv,
    cross_out,
    self_qkv,
    self_out,
    mlp_in,
    mlp_out,
):
    nodes, width = latent.shape
    kv, q, column = project(
        counts.reshape(-1), observations.reshape(-1, width), latent, cross_kv, cross_query,
        mlp_in.T, mlp_out.T,
    )
    weights = lax.all_gather(column, "loc").reshape(-1, *column.shape[1:])
    kv_here, q_here = exchange(kv.reshape(LOC * GROUPS, CAP, 2 * PAIR), q)
    ctx = cross_attention(
        kv_here.reshape(-1, 2 * PAIR), q_here.reshape(-1, PAIR)
    )
    after_cross, self_q, self_kv = middle(
        latent, ctx.reshape(GROUPS, nodes, PAIR), cross_out, self_qkv
    )
    self_ctx = window_attention(self_q, self_kv)
    return tail(self_ctx, after_cross, self_out, weights)


def solution(mesh):
    finer = Mesh(mesh.devices.reshape(LOC, 4, 2), LOC_STREAM)
    return jax.shard_map(
        shards,
        mesh=finer,
        in_specs=(
            P(LOC_STREAM, None),
            P(STREAM, "loc", None, None, None),
            P(STREAM, "loc", None),
            P(),
            P(),
            P(),
            P(),
            P(),
            P(None, LOC_STREAM),
            P(None, LOC_STREAM),
        ),
        out_specs=P(LOC_STREAM, None),
        check_vma=False,
    )
```

profile of v0, /device:TPU:8, one launch (start us, length us, event | category | flops | bytes accessed | tf_op | source)
XLA Modules:
  0.0 158.1 jit_solution(13763987967952626284)
XLA Ops:
  6.5 0.0 all-gather.3.cloned.1.call-start
  6.5 14.9 %project.1 = (bf16[16,8,32,256]{3,2,1,0:T(8,128)(2,1)}, bf16[8,384,128]{2,1,0:T(8,128)(2,1)}, bf16[4,2,32,1024]{3,2,1,0:T(8,128)(2,1)}) custom-call(s32[16]{0:T(128)} %bitcast.15, bf16[512,1024]{1,0:T(8,128)(2,1)} %bitcast.11, bf16[384,1024]{1,0:T(8,128)(2,1)} %latent.3, bf16[1024,2048]{1,0:T(8,128)(2,1)} %wv.1, bf16[1024,2048]{1,0:T(8,128)(2,1)} %wv.1, ...), custom_call_target="tpu_custom_call" | custom-call | tf_op jit(solution)/shard_map/project/pallas_call | solution.py:98
  21.4 0.0 all-gather.3.cloned.1.call-update
  21.5 46.4 %exchange.1 = (bf16[128,32,256]{2,1,0:T(8,128)(2,1)}, bf16[8,384,128]{2,1,0:T(8,128)(2,1)}) custom-call(bf16[128,32,256]{2,1,0:T(8,128)(2,1)} %bitcast.10, bf16[8,384,128]{2,1,0:T(8,128)(2,1)} %get-tuple-element.14.q), custom_call_target="tpu_custom_call" | custom-call | tf_op jit(solution)/shard_map/exchange/pallas_call | solution.py:174
  67.8 20.5 %cross_attention.1 = bf16[3072,128]{1,0:T(8,128)(2,1)} custom-call(bf16[4096,256]{1,0:T(8,128)(2,1)} %bitcast.9, bf16[3072,128]{1,0:T(8,128)(2,1)} %bitcast.12), custom_call_target="tpu_custom_call" | custom-call | tf_op jit(solution)/shard_map/cross_attention/pallas_call | solution.py:453
  88.3 34.7 %middle.1 = (bf16[384,1024]{1,0:T(8,128)(2,1)}, bf16[384,1024]{1,0:T(8,128)(2,1)}, bf16[896,2048]{1,0:T(8,128)(2,1)}) custom-call(bf16[384,1024]{1,0:T(8,128)(2,1)} %latent.3, bf16[8,384,128]{2,1,0:T(8,128)(2,1)} %bitcast.8, bf16[1024,1024]{1,0:T(8,128)(2,1)} %cross_out.1, bf16[1024,3072]{1,0:T(8,128)(2,1)} %self_qkv.1), custom_call_target="tpu_custom_call" | custom-call | tf_op jit(solution)/shard_map/middle/pallas_call | solution.py:316
  123.0 11.8 %window_attention.1.ctx = bf16[384,1024]{1,0:T(8,128)(2,1)} custom-call(bf16[384,1024]{1,0:T(8,128)(2,1)} %get-tuple-element.17.q, bf16[896,2048]{1,0:T(8,128)(2,1)} %get-tuple-element.18.key.value, bf16[896,2048]{1,0:T(8,128)(2,1)} %get-tuple-element.18.key.value), custom_call_target="tpu_custom_call" | custom-call | tf_op jit(solution)/shard_map/window_attention/pallas_call | solution.py:518
  134.8 0.0 all-gather.3.cloned.1.call-done.weights
  134.8 14.5 %tail.1 = bf16[384,1024]{1,0:T(8,128)(2,1)} custom-call(bf16[384,1024]{1,0:T(8,128)(2,1)} %window_attention.1.ctx, bf16[384,1024]{1,0:T(8,128)(2,1)} %get-tuple-element.19.before, bf16[1024,1024]{1,0:T(8,128)(2,1)} %self_out.1, bf16[64,2,32,1024]{3,2,1,0:T(8,128)(2,1)} %all-gather.3.cloned.1.call-done.weights), custom_call_target="tpu_custom_call" | custom-call | tf_op jit(solution)/shard_map/tail/pallas_call | solution.py:606
  149.2 2.1 %copy.12 = bf16[384,1024]{1,0:T(8,128)(2,1)} copy(bf16[384,1024]{1,0:T(8,128)(2,1)} %tail.1) | data formatting | bytes 1572864
Async XLA Ops:
  6.5 128.2 %all-gather.3.cloned.1.call-start = ((), (), s32[]{:S(2)}) async-start(), calls=%async_computation | async-start | bytes 8912896 | tf_op jit(solution)/shard_map/all_gather | solution.py:646
Sparse Core Ops, SparseCore 0:
  21.6 88.5 all-gather.2
where the time goes:
time: 159 us; the launch traced here: 158 us
  Pallas kernels  143 us (90%)
  between operations  13.4 us (8%)
  local copies, waits for them, and re-layouts  2.06 us (1%)
    pallas_call x1, Pallas kernels, exchange(): pl.pallas_call(exchange_kernel, out_shape=(jax.ShapeDtypeStruct(kv.shape,...  46.4 us
    pallas_call x1, Pallas kernels, middle(): pl.pallas_call(middle_kernel, out_shape=(jax.ShapeDtypeStruct((nodes, wid...  34.7 us
    pallas_call x1, Pallas kernels, cross_attention(): pl.pallas_call(cross_kernel, grid=(nodes // block,), out_shape=jax.ShapeD...  20.5 us
    pallas_call x1, Pallas kernels, project(): pl.pallas_call(project_kernel, grid=(steps,), out_shape=(jax.ShapeDtypeSt...  14.9 us
    pallas_call x1, Pallas kernels, tail(): pl.pallas_call(tail_kernel, out_shape=jax.ShapeDtypeStruct(ctx.shape, BF1...  14.5 us
    pallas_call x1, Pallas kernels, window_attention(): pl.pallas_call(functools.partial(window_kernel, block), grid=(GROUPS,), o...  11.8 us
  transfers between devices with their start and end apart: 1, of which 0 were waited for; matrix products, arithmetic and copies ran while one was open for 0% of the time, Pallas kernels for 72%

commit v1 on v0

--- a/solution.py
+++ b/solution.py
@@ -187,13 +187,14 @@
 
 def middle_kernel(
     latent, ctx, cross_out, self_qkv, after, q, kv,
-    mixed, w_out, w_qkv, low, high, normed, w_sems, ctx_send, ctx_recv, send, recv,
+    mixed, w_out, w_qkv, halo, normed, w_sems, ctx_send, ctx_recv, send, recv,
 ):
     loc = lax.axis_index("loc")
     me = lax.axis_index("s0") * 2 + lax.axis_index("s1")
     flat = loc * GROUPS + me
     nodes, width = latent.shape
-    half = low.shape[0]
+    half = halo.shape[1]
+    low, high = halo.at[0], halo.at[1]
     starts, ends = flat == 0, flat == LOC * GROUPS - 1
     outer_low = (me == 0) & jnp.logical_not(starts)
     outer_high = (me == GROUPS - 1) & jnp.logical_not(ends)
@@ -246,11 +247,11 @@
 
     @pl.when(starts)
     def _():
-        low[...] = jnp.zeros_like(low)
+        halo[0] = jnp.zeros(halo.shape[1:], BF16)
 
     @pl.when(ends)
     def _():
-        high[...] = jnp.zeros_like(high)
+        halo[1] = jnp.zeros(halo.shape[1:], BF16)
 
     load_out.wait()
     pltpu.make_async_copy(mixed, mixed, ctx_recv).wait()
@@ -288,19 +289,20 @@
 
     project(normed, slice(half, half + nodes))
 
-    @pl.when(jnp.logical_not(starts))
-    def _():
-        pltpu.make_async_copy(low, low, recv.at[0]).wait()
-
-    normed[0:half] = rms_norm(low[...])
-    project(normed.at[0:half], slice(0, half))
-
-    @pl.when(jnp.logical_not(ends))
-    def _():
-        pltpu.make_async_copy(high, high, recv.at[1]).wait()
-
-    normed[0:half] = rms_norm(high[...])
-    project(normed.at[0:half], slice(half + nodes, 2 * half + nodes))
+    core = lax.axis_index("s1")
+
+    @pl.loop(0, 2)
+    def _(i):
+        side = lax.rem(1 - core + i, 2)
+        come = ((side == 0) & jnp.logical_not(starts)) | ((side == 1) & jnp.logical_not(ends))
+
+        @pl.when(come)
+        def _():
+            pltpu.make_async_copy(halo.at[side], halo.at[side], recv.at[side]).wait()
+
+        normed[0:half] = rms_norm(halo[side])
+        first = pl.multiple_of(side * (half + nodes), PAIR)
+        project(normed.at[0:half], pl.ds(first, half))
 
     pl.when(jnp.logical_not(starts))(down.wait_send)
     pl.when(jnp.logical_not(ends))(up.wait_send)
@@ -326,8 +328,7 @@
             pltpu.VMEM((nodes, width), BF16),
             pltpu.VMEM((width, width), BF16),
             pltpu.VMEM((width, 3 * width), BF16),
-            pltpu.VMEM((half, width), BF16),
-            pltpu.VMEM((half, width), BF16),
+            pltpu.VMEM((2, half, width), BF16),
             pltpu.VMEM((nodes, width), BF16),
             pltpu.SemaphoreType.DMA((2,)),
             pltpu.SemaphoreType.DMA,

time: 159 us -> 157 us (0.987)
  Pallas kernels: 143 us -> 141 us
    pallas_call x1, Pallas kernels: 34.7 us -> 32.7 us  [middle(): pl.pallas_call(middle_kernel, out_shape=(jax.ShapeDtypeStruct((nodes, wid...]
  transfers between devices with their start and end apart: 1 -> 1, of which waited for: 0 -> 0; matrix products, arithmetic and copies ran while one was open for 0% -> 0% of each run, Pallas kernels for 72% -> 71%
where the time goes in v1:
time: 157 us; the launch traced here: 156 us
  Pallas kernels  141 us (90%)
  between operations  13.4 us (9%)
  local copies, waits for them, and re-layouts  2.06 us (1%)
    pallas_call x1, Pallas kernels, exchange(): pl.pallas_call(exchange_kernel, out_shape=(jax.ShapeDtypeStruct(kv.shape,...  46.4 us
    pallas_call x1, Pallas kernels, middle(): pl.pallas_call(middle_kernel, out_shape=(jax.ShapeDtypeStruct((nodes, wid...  32.7 us
    pallas_call x1, Pallas kernels, cross_attention(): pl.pallas_call(cross_kernel, grid=(nodes // block,), out_shape=jax.ShapeD...  20.5 us
    pallas_call x1, Pallas kernels, project(): pl.pallas_call(project_kernel, grid=(steps,), out_shape=(jax.ShapeDtypeSt...  14.9 us
    pallas_call x1, Pallas kernels, tail(): pl.pallas_call(tail_kernel, out_shape=jax.ShapeDtypeStruct(ctx.shape, BF1...  14.5 us
    pallas_call x1, Pallas kernels, window_attention(): pl.pallas_call(functools.partial(window_kernel, block), grid=(GROUPS,), o...  11.8 us
  transfers between devices with their start and end apart: 1, of which 0 were waited for; matrix products, arithmetic and copies ran while one was open for 0% of the time, Pallas kernels for 71%

profile of v1, /device:TPU:8, one launch (start us, length us, event | category | flops | bytes accessed | tf_op | source)
XLA Modules:
  0.0 156.2 jit_solution(16603103307769674162)
XLA Ops:
  6.5 0.0 all-gather.3.cloned.1.call-start
  6.5 14.9 %project.1 = (bf16[16,8,32,256]{3,2,1,0:T(8,128)(2,1)}, bf16[8,384,128]{2,1,0:T(8,128)(2,1)}, bf16[4,2,32,1024]{3,2,1,0:T(8,128)(2,1)}) custom-call(s32[16]{0:T(128)} %bitcast.15, bf16[512,1024]{1,0:T(8,128)(2,1)} %bitcast.11, bf16[384,1024]{1,0:T(8,128)(2,1)} %latent.3, bf16[1024,2048]{1,0:T(8,128)(2,1)} %wv.1, bf16[1024,2048]{1,0:T(8,128)(2,1)} %wv.1, ...), custom_call_target="tpu_custom_call" | custom-call | tf_op jit(solution)/shard_map/project/pallas_call | solution.py:98
  21.4 0.0 all-gather.3.cloned.1.call-update
  21.5 46.4 %exchange.1 = (bf16[128,32,256]{2,1,0:T(8,128)(2,1)}, bf16[8,384,128]{2,1,0:T(8,128)(2,1)}) custom-call(bf16[128,32,256]{2,1,0:T(8,128)(2,1)} %bitcast.10, bf16[8,384,128]{2,1,0:T(8,128)(2,1)} %get-tuple-element.14.q), custom_call_target="tpu_custom_call" | custom-call | tf_op jit(solution)/shard_map/exchange/pallas_call | solution.py:174
  67.8 20.5 %cross_attention.1 = bf16[3072,128]{1,0:T(8,128)(2,1)} custom-call(bf16[4096,256]{1,0:T(8,128)(2,1)} %bitcast.9, bf16[3072,128]{1,0:T(8,128)(2,1)} %bitcast.12), custom_call_target="tpu_custom_call" | custom-call | tf_op jit(solution)/shard_map/cross_attention/pallas_call | solution.py:454
  88.3 32.7 %middle.1 = (bf16[384,1024]{1,0:T(8,128)(2,1)}, bf16[384,1024]{1,0:T(8,128)(2,1)}, bf16[896,2048]{1,0:T(8,128)(2,1)}) custom-call(bf16[384,1024]{1,0:T(8,128)(2,1)} %latent.3, bf16[8,384,128]{2,1,0:T(8,128)(2,1)} %bitcast.8, bf16[1024,1024]{1,0:T(8,128)(2,1)} %cross_out.1, bf16[1024,3072]{1,0:T(8,128)(2,1)} %self_qkv.1), custom_call_target="tpu_custom_call" | custom-call | tf_op jit(solution)/shard_map/middle/pallas_call | solution.py:318
  121.0 11.8 %window_attention.1.ctx = bf16[384,1024]{1,0:T(8,128)(2,1)} custom-call(bf16[384,1024]{1,0:T(8,128)(2,1)} %get-tuple-element.17.q, bf16[896,2048]{1,0:T(8,128)(2,1)} %get-tuple-element.18.key.value, bf16[896,2048]{1,0:T(8,128)(2,1)} %get-tuple-element.18.key.value), custom_call_target="tpu_custom_call" | custom-call | tf_op jit(solution)/shard_map/window_attention/pallas_call | solution.py:519
  132.8 0.0 all-gather.3.cloned.1.call-done.weights
  132.8 14.5 %tail.1 = bf16[384,1024]{1,0:T(8,128)(2,1)} custom-call(bf16[384,1024]{1,0:T(8,128)(2,1)} %window_attention.1.ctx, bf16[384,1024]{1,0:T(8,128)(2,1)} %get-tuple-element.19.before, bf16[1024,1024]{1,0:T(8,128)(2,1)} %self_out.1, bf16[64,2,32,1024]{3,2,1,0:T(8,128)(2,1)} %all-gather.3.cloned.1.call-done.weights), custom_call_target="tpu_custom_call" | custom-call | tf_op jit(solution)/shard_map/tail/pallas_call | solution.py:607
  147.3 2.1 %copy.12 = bf16[384,1024]{1,0:T(8,128)(2,1)} copy(bf16[384,1024]{1,0:T(8,128)(2,1)} %tail.1) | data formatting | bytes 1572864
Async XLA Ops:
  6.5 126.3 %all-gather.3.cloned.1.call-start = ((), (), s32[]{:S(2)}) async-start(), calls=%async_computation | async-start | bytes 8912896 | tf_op jit(solution)/shard_map/all_gather | solution.py:647
Sparse Core Ops, SparseCore 0:
  21.6 88.5 all-gather.2
